TPU v7x, 32 devices: a whole 2x2x4 slice. The times are simulated.
32 devices in a mesh: fsdp: 2 (over x), context: 4 (over z), tensor: 4 (over y, core).
Axes of the slice: x: 2, y: 2, z: 4, core: 2. Of those that a mesh axis runs over, the one named last changes fastest.
Arguments:
- inputs: bfloat16 [4096, 1536], P(('fsdp', 'context')), may hold values from -6 to 6
- cotangent: bfloat16 [4096, 1536], P(('fsdp', 'context')), may hold values from -6 to 6
- blocks: int32 [2, 8], P('fsdp'), may hold values from 0 to 7, each once within a row
- attn_gain: bfloat16 [1536], P('fsdp'), may hold values from 0.25 to 1.75
- w_query: bfloat16 [1536, 1536], P('fsdp', 'tensor'), may hold values from -0.21875 to 0.21875
- b_query: bfloat16 [12, 128], P('tensor', 'fsdp'), may hold values from -3 to 3
- w_key: bfloat16 [1536, 256], P('fsdp'), may hold values from -0.21875 to 0.21875
- b_key: bfloat16 [2, 128], P(None, 'fsdp'), may hold values from -3 to 3
- w_value: bfloat16 [1536, 256], P('fsdp'), may hold values from -0.15625 to 0.15625
- b_value: bfloat16 [2, 128], P(None, 'fsdp'), may hold values from -3 to 3
- w_out: bfloat16 [1536, 1536], P('tensor', 'fsdp'), may hold values from -1 to 1
- ffn_gain: bfloat16 [1536], P('fsdp'), may hold values from 0.25 to 1.75
- w_gate: bfloat16 [1536, 8960], P('fsdp', 'tensor'), may hold values from -0.15625 to 0.15625
- w_up: bfloat16 [1536, 8960], P('fsdp', 'tensor'), may hold values from -0.15625 to 0.15625
- w_down: bfloat16 [8960, 1536], P('tensor', 'fsdp'), may hold values from -0.09375 to 0.09375
Outputs:
- outputs: bfloat16 [4096, 1536], P(('fsdp', 'context'))
- input_grad: bfloat16 [4096, 1536], P(('fsdp', 'context'))
- attn_gain_grad: float32 [1536], P('fsdp')
- w_query_grad: float32 [1536, 1536], P('fsdp', 'tensor')
- b_query_grad: float32 [12, 128], P('tensor', 'fsdp')
- w_key_grad: float32 [1536, 256], P('fsdp')
- b_key_grad: float32 [2, 128], P(None, 'fsdp')
- w_value_grad: float32 [1536, 256], P('fsdp')
- b_value_grad: float32 [2, 128], P(None, 'fsdp')
- w_out_grad: float32 [1536, 1536], P('tensor', 'fsdp')
- ffn_gain_grad: float32 [1536], P('fsdp')
- w_gate_grad: float32 [1536, 8960], P('fsdp', 'tensor')
- w_up_grad: float32 [1536, 8960], P('fsdp', 'tensor')
- w_down_grad: float32 [8960, 1536], P('tensor', 'fsdp')
Inputs may be any that keep to these rules, and one draw needn't show every extreme that they name: `blocks`: each row lists every block number of 0 to 7 once.
All inputs are finite; a program needn't handle non-finite values.
Results may differ from a plain program's by a relative error of at most 0.02.
Values may be sent and summed in bfloat16 or wider, within the bound.
A program may use at most 192 MiB of HBM per device.

v0:
```python
import jax
import jax.numpy as jnp
from jax import lax
from jax.sharding import PartitionSpec as P

H = 12
KV = 2
HD = 128
BLOCK = 256
EPSILON = 1e-06
ROPE_BASE = 1000000.0
MASKED = -1e30


def rope_tables(positions):
    halfway = HD // 2
    frequency = ROPE_BASE ** (-(jnp.arange(halfway, dtype=jnp.float32) * 2.0 / HD))
    angles = positions.astype(jnp.float32)[:, None] * frequency[None, :]
    cosine = jnp.concatenate([jnp.cos(angles), jnp.cos(angles)], axis=1)
    sine = jnp.concatenate([jnp.sin(angles), jnp.sin(angles)], axis=1)
    return (cosine, sine)


def rotate(field, cosine, sine):
    halfway = HD // 2
    turned = jnp.concatenate([-field[..., halfway:], field[..., :halfway]], axis=-1)
    return field * cosine[:, None, :] + turned * sine[:, None, :]


def rotate_back(grad_field, cosine, sine):
    halfway = HD // 2
    moved = grad_field * sine[:, None, :]
    turned = jnp.concatenate([moved[..., halfway:], -moved[..., :halfway]], axis=-1)
    return grad_field * cosine[:, None, :] + turned


def rms_scale(values):
    return lax.rsqrt(jnp.mean(values * values, axis=-1, keepdims=True) + EPSILON)


def norm_back(values, factor, gain, grad_normed):
    gained = gain * grad_normed
    inner = jnp.mean(gained * values, axis=-1, keepdims=True)
    grad_values = factor * gained - values * (factor * factor * factor) * inner
    return (grad_values, jnp.sum(grad_normed * values * factor, axis=0))


def contract_rows(left, right):
    return lax.dot_general(
        left, right, (((0,), (0,)), ((), ())), preferred_element_type=jnp.float32
    )


def contract_cols(left, right):
    return lax.dot_general(
        left, right, (((1,), (1,)), ((), ())), preferred_element_type=jnp.float32
    )


def local(
    inputs,
    cotangent,
    blocks,
    attn_gain,
    w_query,
    b_query,
    w_key,
    b_key,
    w_value,
    b_value,
    w_out,
    ffn_gain,
    w_gate,
    w_up,
    w_down,
):
    rows_here = inputs.shape[0]
    context_index = lax.axis_index("context")
    tensor_index = lax.axis_index("tensor")
    gain_first, wq_all, bq_all, wk_all, bk_all, wv_all, bv_all, wo_all = (
        lax.all_gather(attn_gain, "fsdp", axis=0, tiled=True),
        lax.all_gather(w_query, "fsdp", axis=0, tiled=True),
        lax.all_gather(b_query, "fsdp", axis=1, tiled=True),
        lax.all_gather(w_key, "fsdp", axis=0, tiled=True),
        lax.all_gather(b_key, "fsdp", axis=1, tiled=True),
        lax.all_gather(w_value, "fsdp", axis=0, tiled=True),
        lax.all_gather(b_value, "fsdp", axis=1, tiled=True),
        lax.all_gather(w_out, "fsdp", axis=1, tiled=True),
    )
    seq_blocks = blocks[0]
    seq_length = seq_blocks.shape[0] * BLOCK
    block_of_row = jnp.repeat(seq_blocks, BLOCK, total_repeat_length=seq_length)
    key_positions = block_of_row * BLOCK + jnp.arange(seq_length, dtype=jnp.int32) % BLOCK
    my_blocks = lax.dynamic_slice_in_dim(block_of_row, context_index * rows_here, rows_here)
    my_positions = lax.dynamic_slice_in_dim(key_positions, context_index * rows_here, rows_here)
    cosine, sine = rope_tables(my_positions)
    allowed = block_of_row[None, :] <= my_blocks[:, None]
    inputs_f = inputs.astype(jnp.float32)
    factor_first = rms_scale(inputs_f)
    gain_first_f = gain_first.astype(jnp.float32)
    normed = (inputs_f * factor_first * gain_first_f).astype(jnp.bfloat16)
    query_pre = jnp.dot(normed, wq_all, preferred_element_type=jnp.float32).reshape(
        rows_here, -1, HD
    ) + bq_all.astype(jnp.float32)
    key_pre = jnp.dot(normed, wk_all, preferred_element_type=jnp.float32).reshape(
        rows_here, KV, HD
    ) + bk_all.astype(jnp.float32)
    value_pre = jnp.dot(normed, wv_all, preferred_element_type=jnp.float32).reshape(
        rows_here, KV, HD
    ) + bv_all.astype(jnp.float32)
    queries = rotate(query_pre, cosine, sine).astype(jnp.bfloat16)
    keys = rotate(key_pre, cosine, sine).astype(jnp.bfloat16)
    values = value_pre.astype(jnp.bfloat16)
    key_whole, value_whole = (
        lax.all_gather(keys, "context", axis=0, tiled=True),
        lax.all_gather(values, "context", axis=0, tiled=True),
    )
    heads_here = queries.shape[1]
    group_size = H // KV
    scaling = HD ** (-0.5)
    attended_list = []
    log_totals = []
    for head_slot in range(heads_here):
        key_group = (tensor_index * heads_here + head_slot) // group_size
        key_head = lax.dynamic_index_in_dim(key_whole, key_group, 1, keepdims=False)
        value_head = lax.dynamic_index_in_dim(value_whole, key_group, 1, keepdims=False)
        raw_scores = (
            jnp.einsum(
                "qd,kd->qk", queries[:, head_slot], key_head, preferred_element_type=jnp.float32
            )
            * scaling
        )
        scores = jnp.where(allowed, raw_scores, MASKED)
        row_max = jnp.max(scores, axis=1, keepdims=True)
        expo = jnp.exp(scores - row_max)
        total = jnp.sum(expo, axis=1, keepdims=True)
        probability = (expo / total).astype(jnp.bfloat16)
        attended_list.append(jnp.dot(probability, value_head, preferred_element_type=jnp.float32))
        log_totals.append(row_max + jnp.log(total))
    attended = jnp.concatenate(attended_list, axis=1).astype(jnp.bfloat16)
    attn_part = jnp.dot(attended, wo_all, preferred_element_type=jnp.float32)
    middle = inputs_f + lax.psum(attn_part, "tensor")
    gain_second, wg_all, wu_all, wd_all = (
        lax.all_gather(ffn_gain, "fsdp", axis=0, tiled=True),
        lax.all_gather(w_gate, "fsdp", axis=0, tiled=True),
        lax.all_gather(w_up, "fsdp", axis=0, tiled=True),
        lax.all_gather(w_down, "fsdp", axis=1, tiled=True),
    )
    factor_second = rms_scale(middle)
    gain_second_f = gain_second.astype(jnp.float32)
    normed2 = (middle * factor_second * gain_second_f).astype(jnp.bfloat16)
    gate_pre = jnp.dot(normed2, wg_all, preferred_element_type=jnp.float32)
    up_pre = jnp.dot(normed2, wu_all, preferred_element_type=jnp.float32)
    sigma = jax.nn.sigmoid(gate_pre)
    hidden = (gate_pre * sigma * up_pre).astype(jnp.bfloat16)
    ffn_part = jnp.dot(hidden, wd_all, preferred_element_type=jnp.float32)
    final = middle + lax.psum(ffn_part.astype(jnp.bfloat16), "tensor").astype(jnp.float32)
    outputs = final.astype(jnp.bfloat16)
    grad_out = cotangent.astype(jnp.float32)
    wd_grad = contract_rows(hidden, cotangent)
    grad_hidden = contract_cols(cotangent, wd_all)
    grad_gate = (grad_hidden * up_pre * (sigma + gate_pre * sigma * (1.0 - sigma))).astype(
        jnp.bfloat16
    )
    grad_upper = (grad_hidden * gate_pre * sigma).astype(jnp.bfloat16)
    wg_grad = contract_rows(normed2, grad_gate)
    wu_grad = contract_rows(normed2, grad_upper)
    normed2_part = contract_cols(grad_gate, wg_all) + contract_cols(grad_upper, wu_all)
    grad_normed2 = lax.psum(normed2_part, "tensor")
    grad_mid_norm, ffn_gain_grad = norm_back(middle, factor_second, gain_second_f, grad_normed2)
    grad_middle = grad_out + grad_mid_norm
    grad_middle_low = grad_middle.astype(jnp.bfloat16)
    wo_grad = contract_rows(attended, grad_middle_low)
    grad_attended = contract_cols(grad_middle_low, wo_all).astype(jnp.bfloat16)
    key_grad = jnp.zeros((seq_length, KV, HD), jnp.float32)
    value_grad = jnp.zeros((seq_length, KV, HD), jnp.float32)
    query_grads = []
    for head_slot in range(heads_here):
        key_group = (tensor_index * heads_here + head_slot) // group_size
        key_head = lax.dynamic_index_in_dim(key_whole, key_group, 1, keepdims=False)
        value_head = lax.dynamic_index_in_dim(value_whole, key_group, 1, keepdims=False)
        query_head = queries[:, head_slot]
        raw_scores = (
            jnp.einsum("qd,kd->qk", query_head, key_head, preferred_element_type=jnp.float32)
            * scaling
        )
        scores = jnp.where(allowed, raw_scores, MASKED)
        probability = jnp.exp(scores - log_totals[head_slot])
        prob_low = probability.astype(jnp.bfloat16)
        grad_head = grad_attended[:, head_slot * HD : (head_slot + 1) * HD]
        grad_probs = jnp.einsum(
            "qd,kd->qk", grad_head, value_head, preferred_element_type=jnp.float32
        )
        inner = jnp.sum(probability * grad_probs, axis=1, keepdims=True)
        grad_scores = (probability * (grad_probs - inner)).astype(jnp.bfloat16)
        query_grads.append(
            jnp.dot(grad_scores, key_head, preferred_element_type=jnp.float32) * scaling
        )
        key_piece = contract_rows(grad_scores, query_head) * scaling
        value_piece = contract_rows(prob_low, grad_head)
        select = (jnp.arange(KV, dtype=jnp.int32) == key_group)[None, :, None]
        key_grad = key_grad + jnp.where(select, key_piece[:, None, :], 0.0)
        value_grad = value_grad + jnp.where(select, value_piece[:, None, :], 0.0)
    key_share, value_share = (
        lax.psum_scatter(key_grad, "context", scatter_dimension=0, tiled=True),
        lax.psum_scatter(value_grad, "context", scatter_dimension=0, tiled=True),
    )
    query_grad = jnp.stack(query_grads, axis=1)
    query_low = rotate_back(query_grad, cosine, sine).astype(jnp.bfloat16)
    flat_query = query_low.reshape(rows_here, -1)
    normed_part = contract_cols(flat_query, wq_all)
    grad_normed_query, key_total, value_total = lax.psum(
        (normed_part, key_share, value_share), "tensor"
    )
    key_low = rotate_back(key_total, cosine, sine).astype(jnp.bfloat16)
    value_low = value_total.astype(jnp.bfloat16)
    flat_key = key_low.reshape(rows_here, -1)
    flat_value = value_low.reshape(rows_here, -1)
    grad_normed = (
        grad_normed_query + contract_cols(flat_key, wk_all) + contract_cols(flat_value, wv_all)
    )
    grad_in_norm, attn_gain_grad = norm_back(inputs_f, factor_first, gain_first_f, grad_normed)
    input_grad = (grad_middle + grad_in_norm).astype(jnp.bfloat16)
    wq_grad = contract_rows(normed, flat_query)
    bq_grad = jnp.sum(query_low.astype(jnp.float32), axis=0)
    wk_grad = contract_rows(normed, flat_key)
    bk_grad = jnp.sum(key_low.astype(jnp.float32), axis=0)
    wv_grad = contract_rows(normed, flat_value)
    bv_grad = jnp.sum(value_low.astype(jnp.float32), axis=0)
    pieces = (
        lax.psum_scatter(
            attn_gain_grad.astype(jnp.bfloat16),
            ("fsdp", "context"),
            scatter_dimension=0,
            tiled=True,
        ).astype(jnp.float32),
        lax.psum_scatter(
            wq_grad.astype(jnp.bfloat16), ("fsdp", "context"), scatter_dimension=0, tiled=True
        ).astype(jnp.float32),
        lax.psum_scatter(
            bq_grad.astype(jnp.bfloat16), ("fsdp", "context"), scatter_dimension=1, tiled=True
        ).astype(jnp.float32),
        lax.psum_scatter(
            wk_grad.astype(jnp.bfloat16), ("fsdp", "context"), scatter_dimension=0, tiled=True
        ).astype(jnp.float32),
        lax.psum_scatter(
            bk_grad.astype(jnp.bfloat16), ("fsdp", "context"), scatter_dimension=1, tiled=True
        ).astype(jnp.float32),
        lax.psum_scatter(
            wv_grad.astype(jnp.bfloat16), ("fsdp", "context"), scatter_dimension=0, tiled=True
        ).astype(jnp.float32),
        lax.psum_scatter(
            bv_grad.astype(jnp.bfloat16), ("fsdp", "context"), scatter_dimension=1, tiled=True
        ).astype(jnp.float32),
        lax.psum_scatter(
            wo_grad.astype(jnp.bfloat16), ("fsdp", "context"), scatter_dimension=1, tiled=True
        ).astype(jnp.float32),
        lax.psum_scatter(
            ffn_gain_grad.astype(jnp.bfloat16), ("fsdp", "context"), scatter_dimension=0, tiled=True
        ).astype(jnp.float32),
        lax.psum_scatter(
            wg_grad.astype(jnp.bfloat16), ("fsdp", "context"), scatter_dimension=0, tiled=True
        ).astype(jnp.float32),
        lax.psum_scatter(
            wu_grad.astype(jnp.bfloat16), ("fsdp", "context"), scatter_dimension=0, tiled=True
        ).astype(jnp.float32),
        lax.psum_scatter(
            wd_grad.astype(jnp.bfloat16), ("fsdp", "context"), scatter_dimension=1, tiled=True
        ).astype(jnp.float32),
    )
    shards = (
        lax.all_gather(pieces[0].astype(jnp.bfloat16), "context", axis=0, tiled=True).astype(
            jnp.float32
        ),
        lax.all_gather(pieces[1].astype(jnp.bfloat16), "context", axis=0, tiled=True).astype(
            jnp.float32
        ),
        lax.all_gather(pieces[2].astype(jnp.bfloat16), "context", axis=1, tiled=True).astype(
            jnp.float32
        ),
        lax.all_gather(pieces[3].astype(jnp.bfloat16), "context", axis=0, tiled=True).astype(
            jnp.float32
        ),
        lax.all_gather(pieces[4].astype(jnp.bfloat16), "context", axis=1, tiled=True).astype(
            jnp.float32
        ),
        lax.all_gather(pieces[5].astype(jnp.bfloat16), "context", axis=0, tiled=True).astype(
            jnp.float32
        ),
        lax.all_gather(pieces[6].astype(jnp.bfloat16), "context", axis=1, tiled=True).astype(
            jnp.float32
        ),
        lax.all_gather(pieces[7].astype(jnp.bfloat16), "context", axis=1, tiled=True).astype(
            jnp.float32
        ),
        lax.all_gather(pieces[8].astype(jnp.bfloat16), "context", axis=0, tiled=True).astype(
            jnp.float32
        ),
        lax.all_gather(pieces[9].astype(jnp.bfloat16), "context", axis=0, tiled=True).astype(
            jnp.float32
        ),
        lax.all_gather(pieces[10].astype(jnp.bfloat16), "context", axis=0, tiled=True).astype(
            jnp.float32
        ),
        lax.all_gather(pieces[11].astype(jnp.bfloat16), "context", axis=1, tiled=True).astype(
            jnp.float32
        ),
    )
    return (
        outputs,
        input_grad,
        shards[0],
        shards[1],
        shards[2],
        shards[3],
        shards[4],
        shards[5],
        shards[6],
        shards[7],
        shards[8],
        shards[9],
        shards[10],
        shards[11],
    )


def solution(mesh):
    in_specs = (
        P(("fsdp", "context"), None),
        P(("fsdp", "context"), None),
        P("fsdp", None),
        P("fsdp"),
        P("fsdp", "tensor"),
        P("tensor", "fsdp"),
        P("fsdp", None),
        P(None, "fsdp"),
        P("fsdp", None),
        P(None, "fsdp"),
        P("tensor", "fsdp"),
        P("fsdp"),
        P("fsdp", "tensor"),
        P("fsdp", "tensor"),
        P("tensor", "fsdp"),
    )
    out_specs = (
        P(("fsdp", "context"), None),
        P(("fsdp", "context"), None),
        P("fsdp"),
        P("fsdp", "tensor"),
        P("tensor", "fsdp"),
        P("fsdp", None),
        P(None, "fsdp"),
        P("fsdp", None),
        P(None, "fsdp"),
        P("tensor", "fsdp"),
        P("fsdp"),
        P("fsdp", "tensor"),
        P("fsdp", "tensor"),
        P("tensor", "fsdp"),
    )
    return jax.shard_map(local, mesh=mesh, in_specs=in_specs, out_specs=out_specs, check_vma=False)
```

profile of v0, /device:TPU:0, one launch (start us, length us, event | category | flops | bytes accessed | tf_op | source)
XLA Modules:
  0.0 1892.9 jit_solution(14799244396280470210)
XLA Ops:
  17.9 19.9 %all_gather.81 = bf16[1536,256]{1,0:T(8,128)(2,1)S(1)} all-gather(bf16[768,256]{1,0:T(8,128)(2,1)} %param.23), channel_id=1, replica_groups=mesh['fsdp'=2,'context'=4,'tensor'=4] {'fsdp'}, dimensions={0}, use_global_device_ids=true | all-gather | bytes 1179648 | tf_op jit(solution)/shard_map/all_gather | solution.py:84
  144.6 61.5 %all-reduce.13.cloned.1.call-done = f32[512,1536]{1,0:T(8,128)} async-done(((f32[512,1536]{1,0:T(8,128)}), f32[512,1536]{1,0:T(8,128)}) %all-reduce.13.cloned.1.call-update) | async-done | bytes 3145744 | tf_op jit(solution)/shard_map/psum | solution.py:142
  212.0 82.6 %all-gather.29.cloned.1.call-done = bf16[1536,2240]{0,1:T(8,128)(2,1)} async-done(((bf16[768,2240]{0,1:T(8,128)(2,1)}), bf16[1536,2240]{0,1:T(8,128)(2,1)}) %all-gather.29.cloned.1.call-update) | async-done | bytes 6881296 | tf_op jit(solution)/shard_map/all_gather | solution.py:146
  304.2 79.1 %all-gather.27.cloned.1.call-done = bf16[1536,2240]{0,1:T(8,128)(2,1)} async-done(((bf16[768,2240]{0,1:T(8,128)(2,1)}), bf16[1536,2240]{0,1:T(8,128)(2,1)}) %all-gather.27.cloned.1.call-update) | async-done | bytes 6881296 | tf_op jit(solution)/shard_map/all_gather | solution.py:145
  392.8 79.1 %all-gather.31.cloned.1.call-done = bf16[2240,1536]{1,0:T(8,128)(2,1)} async-done(((bf16[2240,768]{1,0:T(8,128)(2,1)}), bf16[2240,1536]{1,0:T(8,128)(2,1)}) %all-gather.31.cloned.1.call-update) | async-done | bytes 6881296 | tf_op jit(solution)/shard_map/all_gather | solution.py:147
  510.3 56.2 %all-reduce.17.cloned.1.call-done = f32[512,1536]{1,0:T(8,128)} async-done(((f32[512,1536]{1,0:T(8,128)}), f32[512,1536]{1,0:T(8,128)}) %all-reduce.17.cloned.1.call-update) | async-done | bytes 3145744 | tf_op jit(solution)/shard_map/psum | solution.py:169
  570.3 41.9 %all-reduce.15.cloned.1.call-done = bf16[512,1536]{1,0:T(8,128)(2,1)} async-done(((bf16[512,1536]{1,0:T(8,128)(2,1)}), bf16[512,1536]{1,0:T(8,128)(2,1)}) %all-reduce.15.cloned.1.call-update) | async-done | bytes 1572880 | tf_op jit(solution)/shard_map/psum | solution.py:157
  675.0 34.0 %reduce-scatter.19.cloned.1.call-done = f32[512,2,128]{0,2,1:T(8,128)} async-done(((f32[2048,2,128]{0,2,1:T(8,128)}), f32[512,2,128]{0,2,1:T(8,128)}) %reduce-scatter.19.cloned.1.call-update) | async-done | bytes 524304 | tf_op jit(solution)/shard_map/reduce_scatter | solution.py:205
  754.5 23.9 %all-reduce.20 = bf16[512,2,128]{0,2,1:T(8,128)(2,1)} all-reduce(f32[512,2,128]{0,2,1:T(8,128)} %reduce-scatter.21.cloned.1.call-done), channel_id=1, replica_groups=mesh['fsdp'=2,'context'=4,'tensor'=4] {'tensor'}, use_global_device_ids=true, to_apply=%region_19.20 | all-reduce | flops 131072 | bytes 786432 | tf_op jit(solution)/shard_map/psum | solution.py:212
  783.4 54.8 %all-reduce.19.cloned.1.call-done = (f32[512,1536]{1,0:T(8,128)}, f32[512,2,128]{0,2,1:T(8,128)}) async-done(((f32[512,1536]{1,0:T(8,128)}, f32[512,2,128]{0,2,1:T(8,128)}), (f32[512,1536]{1,0:T(8,128)}, f32[512,2,128]{0,2,1:T(8,128)})) %all-reduce.19.cloned.1.call-update) | async-done | bytes 3670032 | tf_op jit(solution)/shard_map/psum | solution.py:212
  844.9 126.1 %reduce-scatter.35.cloned.1.call-done = bf16[2240,192]{0,1:T(8,128)(2,1)} async-done(((bf16[2240,1536]{0,1:T(8,128)(2,1)}), bf16[2240,192]{0,1:T(8,128)(2,1)}) %reduce-scatter.35.cloned.1.call-update) | async-done | bytes 860176 | tf_op jit(solution)/shard_map/reduce_scatter | solution.py:267
  971.0 132.0 %reduce-scatter.31.cloned.1.call-done = bf16[192,2240]{1,0:T(8,128)(2,1)} async-done(((bf16[1536,2240]{1,0:T(8,128)(2,1)}), bf16[192,2240]{1,0:T(8,128)(2,1)}) %reduce-scatter.31.cloned.1.call-update) | async-done | bytes 860176 | tf_op jit(solution)/shard_map/reduce_scatter | solution.py:261
  1103.1 131.5 %reduce-scatter.33.cloned.1.call-done = bf16[192,2240]{1,0:T(8,128)(2,1)} async-done(((bf16[1536,2240]{1,0:T(8,128)(2,1)}), bf16[192,2240]{1,0:T(8,128)(2,1)}) %reduce-scatter.33.cloned.1.call-update) | async-done | bytes 860176 | tf_op jit(solution)/shard_map/reduce_scatter | solution.py:264
  1237.1 53.9 %reduce-scatter.37.cloned.1.call-done = bf16[16,3]{1,0:T(8,128)(2,1)} async-done(((bf16[128,3]{1,0:T(8,128)(2,1)}), bf16[16,3]{1,0:T(8,128)(2,1)}) %reduce-scatter.37.cloned.1.call-update) | async-done | bytes 112
  1302.4 56.1 %reduce-scatter.29.cloned.1.call-done = bf16[384,192]{0,1:T(8,128)(2,1)} async-done(((bf16[384,1536]{0,1:T(8,128)(2,1)}), bf16[384,192]{0,1:T(8,128)(2,1)}) %reduce-scatter.29.cloned.1.call-update) | async-done | bytes 147472 | tf_op jit(solution)/shard_map/reduce_scatter | solution.py:255
  1358.5 17.8 all_gather.99
  1378.6 47.2 %reduce-scatter.23.cloned.1.call-done = bf16[192,384]{1,0:T(8,128)(2,1)} async-done(((bf16[1536,384]{1,0:T(8,128)(2,1)}), bf16[192,384]{1,0:T(8,128)(2,1)}) %reduce-scatter.23.cloned.1.call-update) | async-done | bytes 147472 | tf_op jit(solution)/shard_map/reduce_scatter | solution.py:237
  1443.6 38.0 %reduce-scatter.41.cloned.1.call-done = bf16[16,2]{1,0:T(8,128)(2,1)} async-done(((bf16[128,2]{1,0:T(8,128)(2,1)}), bf16[16,2]{1,0:T(8,128)(2,1)}) %reduce-scatter.41.cloned.1.call-update) | async-done | bytes 80
  1492.8 54.5 %reduce-scatter.27.cloned.1.call-done = bf16[192,256]{1,0:T(8,128)(2,1)} async-done(((bf16[1536,256]{1,0:T(8,128)(2,1)}), bf16[192,256]{1,0:T(8,128)(2,1)}) %reduce-scatter.27.cloned.1.call-update) | async-done | bytes 98320 | tf_op jit(solution)/shard_map/reduce_scatter | solution.py:249
  1569.5 20.2 %all-reduce.5 = (bf16[1536]{0:T(1024)(128)(2,1)S(1)}, bf16[1536]{0:T(1024)(128)(2,1)S(1)}) all-reduce(bf16[1536]{0:T(1024)(128)(2,1)S(1)} %get-tuple-element.84, bf16[1536]{0:T(1024)(128)(2,1)S(1)} %copy-done.40), channel_id=4, replica_groups=mesh['fsdp'=2,'context'=4,'tensor'=4] {'fsdp','context'}, use_global_device_ids=true, to_apply=%region_22.23.clone | all-reduce | flops 3072 | bytes 12288
  1615.1 53.3 %reduce-scatter.25.cloned.1.call-done = bf16[192,256]{1,0:T(8,128)(2,1)} async-done(((bf16[1536,256]{1,0:T(8,128)(2,1)}), bf16[192,256]{1,0:T(8,128)(2,1)}) %reduce-scatter.25.cloned.1.call-update) | async-done | bytes 98320 | tf_op jit(solution)/shard_map/reduce_scatter | solution.py:243
  1685.5 54.4 %all-gather.37.cloned.1.call-done = bf16[2240,768]{0,1:T(8,128)(2,1)} async-done(((bf16[2240,192]{0,1:T(8,128)(2,1)}), bf16[2240,768]{0,1:T(8,128)(2,1)}) %all-gather.37.cloned.1.call-update) | async-done | bytes 3440656 | tf_op jit(solution)/shard_map/all_gather | solution.py:305
  1745.8 64.4 %all-gather.33.cloned.1.call-done = bf16[768,2240]{1,0:T(8,128)(2,1)} async-done(((bf16[192,2240]{1,0:T(8,128)(2,1)}), bf16[768,2240]{1,0:T(8,128)(2,1)}) %all-gather.33.cloned.1.call-update) | async-done | bytes 3440656 | tf_op jit(solution)/shard_map/all_gather | solution.py:299
  1816.0 64.3 %all-gather.35.cloned.1.call-done = bf16[768,2240]{1,0:T(8,128)(2,1)} async-done(((bf16[192,2240]{1,0:T(8,128)(2,1)}), bf16[768,2240]{1,0:T(8,128)(2,1)}) %all-gather.35.cloned.1.call-update) | async-done | bytes 3440656 | tf_op jit(solution)/shard_map/all_gather | solution.py:302
  (328 shorter events, 429.5 us)
Async XLA Ops:
  8.0 72.2 %all-gather.21.cloned.1.call-start = ((), (), s32[]{:S(2)}) async-start(), calls=%async_computation.13 | async-start | bytes 1310720 | tf_op jit(solution)/shard_map/all_gather | solution.py:115
  65.1 68.5 %all-gather.25.cloned.1.call-start = ((), (), s32[]{:S(2)}) async-start(), calls=%async_computation.15 | async-start | bytes 1769472 | tf_op jit(solution)/shard_map/all_gather | solution.py:88
  65.7 140.4 %all-reduce.13.cloned.1.call-start = ((), (), s32[]{:S(2)}) async-start(), calls=%async_computation.16 | async-start | bytes 6291456 | tf_op jit(solution)/shard_map/psum | solution.py:142
  137.5 157.2 %all-gather.29.cloned.1.call-start = ((), (), s32[]{:S(2)}) async-start(), calls=%async_computation.18 | async-start | bytes 10321920 | tf_op jit(solution)/shard_map/all_gather | solution.py:146
  138.1 245.2 %all-gather.27.cloned.1.call-start = ((), (), s32[]{:S(2)}) async-start(), calls=%async_computation.17 | async-start | bytes 10321920 | tf_op jit(solution)/shard_map/all_gather | solution.py:145
  138.9 333.0 %all-gather.31.cloned.1.call-start = ((), (), s32[]{:S(2)}) async-start(), calls=%async_computation.19 | async-start | bytes 10321920 | tf_op jit(solution)/shard_map/all_gather | solution.py:147
  139.6 426.8 %all-reduce.17.cloned.1.call-start = ((), (), s32[]{:S(2)}) async-start(), calls=%async_computation.21 | async-start | bytes 6291456 | tf_op jit(solution)/shard_map/psum | solution.py:169
  497.8 114.4 %all-reduce.15.cloned.1.call-start = ((), (), s32[]{:S(2)}) async-start(), calls=%async_computation.20 | async-start | bytes 3145728 | tf_op jit(solution)/shard_map/psum | solution.py:157
  509.3 199.7 %reduce-scatter.19.cloned.1.call-start = ((), (), s32[]{:S(2)}) async-start(), calls=%async_computation.22 | async-start | bytes 2621440 | tf_op jit(solution)/shard_map/reduce_scatter | solution.py:205
  664.9 89.6 %reduce-scatter.21.cloned.1.call-start = ((), (), s32[]{:S(2)}) async-start(), calls=%async_computation.23 | async-start | bytes 2621440 | tf_op jit(solution)/shard_map/reduce_scatter | solution.py:206
  665.4 172.8 %all-reduce.19.cloned.1.call-start = ((), (), s32[]{:S(2)}) async-start(), calls=%async_computation.37 | async-start | bytes 7340032 | tf_op jit(solution)/shard_map/psum | solution.py:212
  709.0 261.9 %reduce-scatter.35.cloned.1.call-start = ((), (), s32[]{:S(2)}) async-start(), calls=%async_computation.32 | async-start | bytes 7962624 | tf_op jit(solution)/shard_map/reduce_scatter | solution.py:267
  717.9 385.1 %reduce-scatter.31.cloned.1.call-start = ((), (), s32[]{:S(2)}) async-start(), calls=%async_computation.28 | async-start | bytes 7962624 | tf_op jit(solution)/shard_map/reduce_scatter | solution.py:261
  727.1 507.5 %reduce-scatter.33.cloned.1.call-start = ((), (), s32[]{:S(2)}) async-start(), calls=%async_computation.30 | async-start | bytes 7962624 | tf_op jit(solution)/shard_map/reduce_scatter | solution.py:264
  736.1 554.9 %reduce-scatter.37.cloned.1.call-start = ((), (), s32[]{:S(2)}) async-start(), calls=%async_computation.34 | async-start | bytes 36864
  736.9 621.6 %reduce-scatter.29.cloned.1.call-start = ((), (), s32[]{:S(2)}) async-start(), calls=%async_computation.27 | async-start | bytes 1327104 | tf_op jit(solution)/shard_map/reduce_scatter | solution.py:255
  740.0 685.8 %reduce-scatter.23.cloned.1.call-start = ((), (), s32[]{:S(2)}) async-start(), calls=%async_computation.24 | async-start | bytes 1327104 | tf_op jit(solution)/shard_map/reduce_scatter | solution.py:237
  743.8 737.8 %reduce-scatter.41.cloned.1.call-start = ((), (), s32[]{:S(2)}) async-start(), calls=%async_computation.36 | async-start | bytes 36864
  780.2 767.2 %reduce-scatter.27.cloned.1.call-start = ((), (), s32[]{:S(2)}) async-start(), calls=%async_computation.26 | async-start | bytes 884736 | tf_op jit(solution)/shard_map/reduce_scatter | solution.py:249
  783.4 820.8 %reduce-scatter.39.cloned.1.call-start = ((), (), s32[]{:S(2)}) async-start(), calls=%async_computation.35 | async-start | bytes 36864
  841.4 826.9 %reduce-scatter.25.cloned.1.call-start = ((), (), s32[]{:S(2)}) async-start(), calls=%async_computation.25 | async-start | bytes 884736 | tf_op jit(solution)/shard_map/reduce_scatter | solution.py:243
  844.8 895.1 %all-gather.37.cloned.1.call-start = ((), (), s32[]{:S(2)}) async-start(), calls=%async_computation.33 | async-start | bytes 4423680 | tf_op jit(solution)/shard_map/all_gather | solution.py:305
  971.0 839.2 %all-gather.33.cloned.1.call-start = ((), (), s32[]{:S(2)}) async-start(), calls=%async_computation.29 | async-start | bytes 4423680 | tf_op jit(solution)/shard_map/all_gather | solution.py:299
  1103.0 777.3 %all-gather.35.cloned.1.call-start = ((), (), s32[]{:S(2)}) async-start(), calls=%async_computation.31 | async-start | bytes 4423680 | tf_op jit(solution)/shard_map/all_gather | solution.py:302
  (68 other events, 2006.3 us)
Sparse Core Ops, SparseCore 0:
  9.7 32.0 all-gather.18
  50.4 29.7 all-gather.20
  137.6 68.4 all-reduce.12
  207.5 87.1 all-gather.28
  296.2 87.0 all-gather.26
  384.8 87.0 all-gather.30
  497.9 68.4 all-reduce.16
  569.2 42.9 all-reduce.14
  665.0 43.9 reduce-scatter.18
  711.3 43.1 reduce-scatter.20
  757.5 80.6 all-reduce.18
  841.8 129.0 reduce-scatter.34
  974.9 128.0 reduce-scatter.30
  1106.5 128.0 reduce-scatter.32
  1238.5 52.5 reduce-scatter.36
  1295.2 63.2 reduce-scatter.28
  1362.8 62.9 reduce-scatter.22
  1429.1 52.4 reduce-scatter.40
  1485.8 61.5 reduce-scatter.26
  1550.5 52.4 reduce-scatter.38
  1606.9 61.4 reduce-scatter.24
  1669.9 69.9 all-gather.36
  1741.6 68.5 all-gather.32
  1811.7 68.5 all-gather.34
  (2 shorter events, 49.6 us)
where the time goes:
time: 1900 us; the launch traced here: 1890 us
  waiting for transfers between devices  1420 us (75%)
  blocking collectives  200 us (11%)
  matrix products  147 us (8%)
  local copies, waits for them, and re-layouts  54.8 us (3%)
  other arithmetic  52 us (3%)
    reduce_scatter x1, waiting for transfers between devices, local(): lax.psum_scatter(wg_grad.astype(jnp.bfloat16), ('fsdp', 'context'), scatt...  132 us
    reduce_scatter x1, waiting for transfers between devices, local(): lax.psum_scatter(wu_grad.astype(jnp.bfloat16), ('fsdp', 'context'), scatt...  132 us
    reduce_scatter x1, waiting for transfers between devices, local(): lax.psum_scatter(wd_grad.astype(jnp.bfloat16), ('fsdp', 'context'), scatt...  126 us
    unnamed x29, waiting for transfers between devices  95.9 us
    all_gather x1, waiting for transfers between devices, local(): lax.all_gather(w_up, 'fsdp', axis=0, tiled=True)  82.6 us
    all_gather x1, waiting for transfers between devices, local(): lax.all_gather(w_gate, 'fsdp', axis=0, tiled=True)  79.1 us
    all_gather x1, waiting for transfers between devices, local(): lax.all_gather(w_down, 'fsdp', axis=1, tiled=True)  79.1 us
    all_gather x1, waiting for transfers between devices, local(): lax.all_gather(pieces[9].astype(jnp.bfloat16), 'context', axis=0, tiled=T...  64.4 us
  transfers between devices with their start and end apart: 26, of which 24 were waited for; matrix products, arithmetic and copies ran while one was open for 8% of the time, Pallas kernels for 0%

commit v1 on v0

--- a/solution.py
+++ b/solution.py
@@ -10,6 +10,34 @@
 EPSILON = 1e-06
 ROPE_BASE = 1000000.0
 MASKED = -1e30
+
+
+def pack_rings(panel):
+    across = "context"
+    base_arr, outcome_arr, response = (
+        jax.lax.axis_size(across),
+        jax.lax.axis_index(across),
+        panel.shape[1],
+    )
+    tray = [(k0, (k0 + 1) % base_arr) for k0 in range(base_arr)]
+    steps_seen = [(k0, (k0 - 1) % base_arr) for k0 in range(base_arr)]
+    mat_out = jnp.zeros((*panel.shape[:1], base_arr * response, *panel.shape[2:]), panel.dtype)
+    aux = earlier = panel
+    formed = base_arr // 2
+    mat_out = lax.dynamic_update_slice_in_dim(mat_out, panel, outcome_arr * response, axis=1)
+    jj = 1
+    while jj < formed + 1:
+        aux = jax.lax.ppermute(aux, across, tray)
+        mat_out = lax.dynamic_update_slice_in_dim(
+            mat_out, aux, (outcome_arr - jj) % base_arr * response, axis=1
+        )
+        if jj < base_arr - formed:
+            earlier = jax.lax.ppermute(earlier, across, steps_seen)
+            mat_out = lax.dynamic_update_slice_in_dim(
+                mat_out, earlier, (outcome_arr + jj) % base_arr * response, axis=1
+            )
+        jj += 1
+    return mat_out
 
 
 def rope_tables(positions):
@@ -302,9 +330,7 @@
         lax.all_gather(pieces[10].astype(jnp.bfloat16), "context", axis=0, tiled=True).astype(
             jnp.float32
         ),
-        lax.all_gather(pieces[11].astype(jnp.bfloat16), "context", axis=1, tiled=True).astype(
-            jnp.float32
-        ),
+        pack_rings(pieces[11].astype(jnp.bfloat16)).astype(jnp.float32),
     )
     return (
         outputs,

time: 1900 us -> 1840 us (0.968)
  waiting for transfers between devices: 1420 us -> 1290 us
  local copies, waits for them, and re-layouts: 54.8 us -> 103 us
    all_gather x1, waiting for transfers between devices: 64.4 us -> 0.01 us  [local(): lax.all_gather(pieces[9].astype(jnp.bfloat16), 'context', axis=0, tiled=T...]
    all_gather x1 -> x0, waiting for transfers between devices: 54.4 us -> none  [local(): lax.all_gather(pieces[11].astype(jnp.bfloat16), 'context', axis=1, tiled=...]
    dynamic_update_slice x0 -> x4, local copies, waits for them, and re-layouts: none -> 46.5 us  [the longest x2 22.8 us: pack_rings(): lax.dynamic_update_slice_in_dim(mat_out, aux, (outcome_arr - jj) % base_a...]
    unnamed x29 -> x28, waiting for transfers between devices: 95.9 us -> 105 us
    unnamed x152 -> x155, local copies, waits for them, and re-layouts: 43.4 us -> 37.5 us
  transfers between devices with their start and end apart: 26 -> 28, of which waited for: 24 -> 23; matrix products, arithmetic and copies ran while one was open for 8% -> 12% of each run, Pallas kernels for 0% -> 0%
where the time goes in v1:
time: 1840 us; the launch traced here: 1830 us
  waiting for transfers between devices  1290 us (70%)
  blocking collectives  213 us (12%)
  matrix products  148 us (8%)
  local copies, waits for them, and re-layouts  103 us (6%)
  other arithmetic  59.3 us (3%)
    reduce_scatter x1, waiting for transfers between devices, local(): lax.psum_scatter(wu_grad.astype(jnp.bfloat16), ('fsdp', 'context'), scatt...  132 us
    reduce_scatter x1, waiting for transfers between devices, local(): lax.psum_scatter(wg_grad.astype(jnp.bfloat16), ('fsdp', 'context'), scatt...  126 us
    reduce_scatter x1, waiting for transfers between devices, local(): lax.psum_scatter(wd_grad.astype(jnp.bfloat16), ('fsdp', 'context'), scatt...  117 us
    unnamed x28, waiting for transfers between devices  105 us
    all_gather x1, waiting for transfers between devices, local(): lax.all_gather(w_gate, 'fsdp', axis=0, tiled=True)  82.6 us
    all_gather x1, waiting for transfers between devices, local(): lax.all_gather(w_up, 'fsdp', axis=0, tiled=True)  79.1 us
    all_gather x1, waiting for transfers between devices, local(): lax.all_gather(w_down, 'fsdp', axis=1, tiled=True)  79.1 us
    psum x1, waiting for transfers between devices, local(): middle = inputs_f + lax.psum(attn_part, 'tensor')  61.5 us
  transfers between devices with their start and end apart: 28, of which 23 were waited for; matrix products, arithmetic and copies ran while one was open for 12% of the time, Pallas kernels for 0%

profile of v1, /device:TPU:0, one launch (start us, length us, event | category | flops | bytes accessed | tf_op | source)
XLA Modules:
  0.0 1832.6 jit_solution(1100857927830428637)
XLA Ops:
  83.4 17.4 all-gather.22.cloned.1.call-done
  135.5 61.5 %all-reduce.13.cloned.1.call-done = f32[512,1536]{1,0:T(8,128)} async-done(((f32[512,1536]{1,0:T(8,128)}), f32[512,1536]{1,0:T(8,128)}) %all-reduce.13.cloned.1.call-update) | async-done | bytes 3145744 | tf_op jit(solution)/shard_map/psum | solution.py:170
  202.9 82.6 %all-gather.26.cloned.1.call-done = bf16[1536,2240]{0,1:T(8,128)(2,1)} async-done(((bf16[768,2240]{0,1:T(8,128)(2,1)}), bf16[1536,2240]{0,1:T(8,128)(2,1)}) %all-gather.26.cloned.1.call-update) | async-done | bytes 6881296 | tf_op jit(solution)/shard_map/all_gather | solution.py:173
  295.1 79.1 %all-gather.28.cloned.1.call-done = bf16[1536,2240]{0,1:T(8,128)(2,1)} async-done(((bf16[768,2240]{0,1:T(8,128)(2,1)}), bf16[1536,2240]{0,1:T(8,128)(2,1)}) %all-gather.28.cloned.1.call-update) | async-done | bytes 6881296 | tf_op jit(solution)/shard_map/all_gather | solution.py:174
  383.7 79.1 %all-gather.30.cloned.1.call-done = bf16[2240,1536]{1,0:T(8,128)(2,1)} async-done(((bf16[2240,768]{1,0:T(8,128)(2,1)}), bf16[2240,1536]{1,0:T(8,128)(2,1)}) %all-gather.30.cloned.1.call-update) | async-done | bytes 6881296 | tf_op jit(solution)/shard_map/all_gather | solution.py:175
  503.8 54.2 %all-reduce.17.cloned.1.call-done = f32[512,1536]{1,0:T(8,128)} async-done(((f32[512,1536]{1,0:T(8,128)}), f32[512,1536]{1,0:T(8,128)}) %all-reduce.17.cloned.1.call-update) | async-done | bytes 3145744 | tf_op jit(solution)/shard_map/psum | solution.py:197
  561.8 41.9 %all-reduce.15.cloned.1.call-done = bf16[512,1536]{1,0:T(8,128)(2,1)} async-done(((bf16[512,1536]{1,0:T(8,128)(2,1)}), bf16[512,1536]{1,0:T(8,128)(2,1)}) %all-reduce.15.cloned.1.call-update) | async-done | bytes 1572880 | tf_op jit(solution)/shard_map/psum | solution.py:185
  666.5 33.9 %reduce-scatter.19.cloned.1.call-done = f32[512,2,128]{0,2,1:T(8,128)} async-done(((f32[2048,2,128]{0,2,1:T(8,128)}), f32[512,2,128]{0,2,1:T(8,128)}) %reduce-scatter.19.cloned.1.call-update) | async-done | bytes 524304 | tf_op jit(solution)/shard_map/reduce_scatter | solution.py:233
  726.3 19.7 %reduce-scatter.21.cloned.1.call-done = f32[512,2,128]{0,2,1:T(8,128)} async-done(((f32[2048,2,128]{0,2,1:T(8,128)}), f32[512,2,128]{0,2,1:T(8,128)}) %reduce-scatter.21.cloned.1.call-update) | async-done | bytes 524304 | tf_op jit(solution)/shard_map/reduce_scatter | solution.py:234
  746.0 23.9 %all-reduce.20 = bf16[512,2,128]{0,2,1:T(8,128)(2,1)} all-reduce(f32[512,2,128]{0,2,1:T(8,128)} %reduce-scatter.21.cloned.1.call-done), channel_id=1, replica_groups=mesh['fsdp'=2,'context'=4,'tensor'=4] {'tensor'}, use_global_device_ids=true, to_apply=%region_19.20 | all-reduce | flops 131072 | bytes 786432 | tf_op jit(solution)/shard_map/psum | solution.py:240
  783.8 45.9 %all-reduce.19.cloned.1.call-done = (f32[512,1536]{1,0:T(8,128)}, f32[512,2,128]{0,2,1:T(8,128)}) async-done(((f32[512,1536]{1,0:T(8,128)}, f32[512,2,128]{0,2,1:T(8,128)}), (f32[512,1536]{1,0:T(8,128)}, f32[512,2,128]{0,2,1:T(8,128)})) %all-reduce.19.cloned.1.call-update) | async-done | bytes 3670032 | tf_op jit(solution)/shard_map/psum | solution.py:240
  836.3 126.1 %reduce-scatter.31.cloned.1.call-done = bf16[192,2240]{1,0:T(8,128)(2,1)} async-done(((bf16[1536,2240]{1,0:T(8,128)(2,1)}), bf16[192,2240]{1,0:T(8,128)(2,1)}) %reduce-scatter.31.cloned.1.call-update) | async-done | bytes 860176 | tf_op jit(solution)/shard_map/reduce_scatter | solution.py:289
  962.5 132.0 %reduce-scatter.33.cloned.1.call-done = bf16[192,2240]{1,0:T(8,128)(2,1)} async-done(((bf16[1536,2240]{1,0:T(8,128)(2,1)}), bf16[192,2240]{1,0:T(8,128)(2,1)}) %reduce-scatter.33.cloned.1.call-update) | async-done | bytes 860176 | tf_op jit(solution)/shard_map/reduce_scatter | solution.py:292
  1097.1 53.5 %reduce-scatter.37.cloned.1.call-done = bf16[16,3]{1,0:T(8,128)(2,1)} async-done(((bf16[128,3]{1,0:T(8,128)(2,1)}), bf16[16,3]{1,0:T(8,128)(2,1)}) %reduce-scatter.37.cloned.1.call-update) | async-done | bytes 112
  1162.0 55.6 %reduce-scatter.23.cloned.1.call-done = bf16[192,384]{1,0:T(8,128)(2,1)} async-done(((bf16[1536,384]{1,0:T(8,128)(2,1)}), bf16[192,384]{1,0:T(8,128)(2,1)}) %reduce-scatter.23.cloned.1.call-update) | async-done | bytes 147472 | tf_op jit(solution)/shard_map/reduce_scatter | solution.py:265
  1236.0 48.5 %reduce-scatter.29.cloned.1.call-done = bf16[384,192]{0,1:T(8,128)(2,1)} async-done(((bf16[384,1536]{0,1:T(8,128)(2,1)}), bf16[384,192]{0,1:T(8,128)(2,1)}) %reduce-scatter.29.cloned.1.call-update) | async-done | bytes 147472 | tf_op jit(solution)/shard_map/reduce_scatter | solution.py:283
  1284.5 17.5 all_gather.96
  1304.4 35.9 %reduce-scatter.41.cloned.1.call-done = bf16[16,2]{1,0:T(8,128)(2,1)} async-done(((bf16[128,2]{1,0:T(8,128)(2,1)}), bf16[16,2]{1,0:T(8,128)(2,1)}) %reduce-scatter.41.cloned.1.call-update) | async-done | bytes 80
  1351.5 54.0 %reduce-scatter.27.cloned.1.call-done = bf16[192,256]{1,0:T(8,128)(2,1)} async-done(((bf16[1536,256]{1,0:T(8,128)(2,1)}), bf16[192,256]{1,0:T(8,128)(2,1)}) %reduce-scatter.27.cloned.1.call-update) | async-done | bytes 98320 | tf_op jit(solution)/shard_map/reduce_scatter | solution.py:277
  1422.0 117.0 %reduce-scatter.35.cloned.1.call-done = bf16[2240,192]{0,1:T(8,128)(2,1)} async-done(((bf16[2240,1536]{0,1:T(8,128)(2,1)}), bf16[2240,192]{0,1:T(8,128)(2,1)}) %reduce-scatter.35.cloned.1.call-update) | async-done | bytes 860176 | tf_op jit(solution)/shard_map/reduce_scatter | solution.py:295
  1545.4 28.7 %all-reduce.5 = (bf16[1536]{0:T(1024)(128)(2,1)S(1)}, bf16[1536]{0:T(1024)(128)(2,1)S(1)}) all-reduce(bf16[1536]{0:T(1024)(128)(2,1)S(1)} %get-tuple-element.84, bf16[1536]{0:T(1024)(128)(2,1)S(1)} %copy-done.42), channel_id=4, replica_groups=mesh['fsdp'=2,'context'=4,'tensor'=4] {'fsdp','context'}, use_global_device_ids=true, to_apply=%region_22.23.clone | all-reduce | flops 3072 | bytes 12288
  1604.5 20.5 %all-gather.6 = bf16[4,16,2]{1,2,0:T(2,128)(2,1)S(1)} all-gather(bf16[1,16,2]{1,2,0:T(2,128)(2,1)S(1)} %bitcast.186), channel_id=1, replica_groups=mesh['fsdp'=2,'context'=4,'tensor'=4] {'context'}, dimensions={0}, use_global_device_ids=true | all-gather | bytes 320 | tf_op jit(solution)/shard_map/all_gather | solution.py:312
  1625.6 52.5 %reduce-scatter.25.cloned.1.call-done = bf16[192,256]{1,0:T(8,128)(2,1)} async-done(((bf16[1536,256]{1,0:T(8,128)(2,1)}), bf16[192,256]{1,0:T(8,128)(2,1)}) %reduce-scatter.25.cloned.1.call-update) | async-done | bytes 98320 | tf_op jit(solution)/shard_map/reduce_scatter | solution.py:271
  1762.1 57.9 %all-gather.34.cloned.1.call-done = bf16[768,2240]{1,0:T(8,128)(2,1)} async-done(((bf16[192,2240]{1,0:T(8,128)(2,1)}), bf16[768,2240]{1,0:T(8,128)(2,1)}) %all-gather.34.cloned.1.call-update) | async-done | bytes 3440656 | tf_op jit(solution)/shard_map/all_gather | solution.py:330
  (344 shorter events, 476.9 us)
Async XLA Ops:
  55.9 68.6 %all-gather.24.cloned.1.call-start = ((), (), s32[]{:S(2)}) async-start(), calls=%async_computation.15 | async-start | bytes 1769472 | tf_op jit(solution)/shard_map/all_gather | solution.py:116
  56.5 140.6 %all-reduce.13.cloned.1.call-start = ((), (), s32[]{:S(2)}) async-start(), calls=%async_computation.16 | async-start | bytes 6291456 | tf_op jit(solution)/shard_map/psum | solution.py:170
  128.4 157.2 %all-gather.26.cloned.1.call-start = ((), (), s32[]{:S(2)}) async-start(), calls=%async_computation.17 | async-start | bytes 10321920 | tf_op jit(solution)/shard_map/all_gather | solution.py:173
  129.0 245.2 %all-gather.28.cloned.1.call-start = ((), (), s32[]{:S(2)}) async-start(), calls=%async_computation.18 | async-start | bytes 10321920 | tf_op jit(solution)/shard_map/all_gather | solution.py:174
  129.8 333.0 %all-gather.30.cloned.1.call-start = ((), (), s32[]{:S(2)}) async-start(), calls=%async_computation.19 | async-start | bytes 10321920 | tf_op jit(solution)/shard_map/all_gather | solution.py:175
  130.5 427.5 %all-reduce.17.cloned.1.call-start = ((), (), s32[]{:S(2)}) async-start(), calls=%async_computation.21 | async-start | bytes 6291456 | tf_op jit(solution)/shard_map/psum | solution.py:197
  489.4 114.4 %all-reduce.15.cloned.1.call-start = ((), (), s32[]{:S(2)}) async-start(), calls=%async_computation.20 | async-start | bytes 3145728 | tf_op jit(solution)/shard_map/psum | solution.py:185
  502.3 198.1 %reduce-scatter.19.cloned.1.call-start = ((), (), s32[]{:S(2)}) async-start(), calls=%async_computation.22 | async-start | bytes 2621440 | tf_op jit(solution)/shard_map/reduce_scatter | solution.py:233
  656.4 89.6 %reduce-scatter.21.cloned.1.call-start = ((), (), s32[]{:S(2)}) async-start(), calls=%async_computation.23 | async-start | bytes 2621440 | tf_op jit(solution)/shard_map/reduce_scatter | solution.py:234
  657.0 172.8 %all-reduce.19.cloned.1.call-start = ((), (), s32[]{:S(2)}) async-start(), calls=%async_computation.36 | async-start | bytes 7340032 | tf_op jit(solution)/shard_map/psum | solution.py:240
  700.4 262.0 %reduce-scatter.31.cloned.1.call-start = ((), (), s32[]{:S(2)}) async-start(), calls=%async_computation.28 | async-start | bytes 7962624 | tf_op jit(solution)/shard_map/reduce_scatter | solution.py:289
  709.4 385.2 %reduce-scatter.33.cloned.1.call-start = ((), (), s32[]{:S(2)}) async-start(), calls=%async_computation.30 | async-start | bytes 7962624 | tf_op jit(solution)/shard_map/reduce_scatter | solution.py:292
  718.6 432.1 %reduce-scatter.37.cloned.1.call-start = ((), (), s32[]{:S(2)}) async-start(), calls=%async_computation.33 | async-start | bytes 36864
  719.4 498.2 %reduce-scatter.23.cloned.1.call-start = ((), (), s32[]{:S(2)}) async-start(), calls=%async_computation.24 | async-start | bytes 1327104 | tf_op jit(solution)/shard_map/reduce_scatter | solution.py:265
  723.2 561.4 %reduce-scatter.29.cloned.1.call-start = ((), (), s32[]{:S(2)}) async-start(), calls=%async_computation.27 | async-start | bytes 1327104 | tf_op jit(solution)/shard_map/reduce_scatter | solution.py:283
  726.3 614.0 %reduce-scatter.41.cloned.1.call-start = ((), (), s32[]{:S(2)}) async-start(), calls=%async_computation.35 | async-start | bytes 36864
  771.7 633.8 %reduce-scatter.27.cloned.1.call-start = ((), (), s32[]{:S(2)}) async-start(), calls=%async_computation.26 | async-start | bytes 884736 | tf_op jit(solution)/shard_map/reduce_scatter | solution.py:277
  774.9 764.1 %reduce-scatter.35.cloned.1.call-start = ((), (), s32[]{:S(2)}) async-start(), calls=%async_computation.32 | async-start | bytes 7962624 | tf_op jit(solution)/shard_map/reduce_scatter | solution.py:295
  783.8 819.9 %reduce-scatter.39.cloned.1.call-start = ((), (), s32[]{:S(2)}) async-start(), calls=%async_computation.34 | async-start | bytes 36864
  832.9 845.3 %reduce-scatter.25.cloned.1.call-start = ((), (), s32[]{:S(2)}) async-start(), calls=%async_computation.25 | async-start | bytes 884736 | tf_op jit(solution)/shard_map/reduce_scatter | solution.py:271
  836.3 919.8 %all-gather.32.cloned.1.call-start = ((), (), s32[]{:S(2)}) async-start(), calls=%async_computation.29 | async-start | bytes 4423680 | tf_op jit(solution)/shard_map/all_gather | solution.py:327
  962.5 857.5 %all-gather.34.cloned.1.call-start = ((), (), s32[]{:S(2)}) async-start(), calls=%async_computation.31 | async-start | bytes 4423680 | tf_op jit(solution)/shard_map/all_gather | solution.py:330
  1585.2 138.5 %collective-permute-start.1 = (bf16[2240,192]{0,1:T(8,128)(2,1)}, bf16[2240,192]{0,1:T(8,128)(2,1)}, u32[]{:S(2)}, u32[]{:S(2)}) collective-permute-start(bf16[2240,192]{0,1:T(8,128)(2,1)} %reduce-scatter.35.cloned.1.call-done), channel_id=1, source_target_pairs={{0,12},{4,0},{8,4},{12,8},{1,13},{5,1},{9,5},{13,9},{2,14},{6,2},{... | collective-permute-start | bytes 2580488 | tf_op jit(solution)/shard_map/ppermute | solution.py:35
  1586.2 151.9 %collective-permute-start.2 = (bf16[2240,192]{0,1:T(8,128)(2,1)}, bf16[2240,192]{0,1:T(8,128)(2,1)}, u32[]{:S(2)}, u32[]{:S(2)}) collective-permute-start(bf16[2240,192]{0,1:T(8,128)(2,1)} %collective-permute-done), channel_id=1, source_target_pairs={{0,4},{4,8},{8,12},{12,0},{1,5},{5,9},{9,13},{13,1},{2,6},{6,10},{... | collective-permute-start | bytes 2580488 | tf_op jit(solution)/shard_map/ppermute | solution.py:30
  (72 other events, 1804.5 us)
Sparse Core Ops, SparseCore 0:
  9.7 25.5 all-gather.17
  41.4 29.7 all-gather.19
  73.3 27.4 all-gather.21
  128.6 68.4 all-reduce.12
  198.4 87.1 all-gather.25
  287.1 87.0 all-gather.27
  375.7 87.0 all-gather.29
  489.5 68.4 all-reduce.16
  560.8 42.9 all-reduce.14
  656.5 43.8 reduce-scatter.18
  702.7 43.2 reduce-scatter.20
  749.1 80.6 all-reduce.18
  833.3 129.1 reduce-scatter.30
  966.4 128.0 reduce-scatter.32
  1098.1 52.5 reduce-scatter.36
  1154.5 63.0 reduce-scatter.22
  1221.4 63.0 reduce-scatter.28
  1287.7 52.5 reduce-scatter.40
  1343.9 61.5 reduce-scatter.26
  1409.7 129.3 reduce-scatter.34
  1542.1 61.5 reduce-scatter.38
  1607.6 70.5 reduce-scatter.24
  1679.7 69.9 all-gather.31
  1751.3 68.5 all-gather.33
  (1 shorter events, 22.2 us)
